TPU v7x, 32 devices: a whole 2x2x4 slice. The times are simulated.
32 devices in a mesh: mpo: 4 (over x, core), bond: 8 (over z, y).
Axes of the slice: x: 2, y: 2, z: 4, core: 2. Of those that a mesh axis runs over, the one named last changes fastest.
Arguments:
- environment: bfloat16 [4096, 40, 4096], P(None, 'mpo', 'bond'), may hold values from -60 to 60
- site_tensor: bfloat16 [4096, 4, 4096], P('bond'), may hold values from -0.09375 to 0.09375
- mpo_tensor: bfloat16 [40, 40, 4, 4], replicated, may hold values from -0.5 to 0.5
- sketch_site: bfloat16 [4096, 128], replicated, may hold values from -6 to 6
- sketch_expand: bfloat16 [128, 40, 4096], P('mpo'), may hold values from -60 to 60
- row_sectors: int32 [2, 4096, 4], P(None, 'bond'), may hold values from 0 to 5, as said below
- column_sectors: int32 [2, 128], replicated, may hold values from 0 to 5, as said below
Outputs:
- basis: bfloat16 [4096, 4, 128], P('bond')
- extended: float32 [128, 40, 128], P('bond', 'mpo')
Inputs may be any that keep to these rules, and one draw needn't show every extreme that they name: `row_sectors`: every joined row's label pair is (4, 0) or (5, 1); the rows labelled (5, 1) are one run of 64 consecutive joined rows (a, s) in the order a then s. `column_sectors`: every column's label pair is (4, 0) or (5, 1); exactly 16 columns are labelled (5, 1).
All inputs are finite; a program needn't handle non-finite values.
Results may differ from a plain program's by a relative error of at most 0.0064.
Values may be sent and summed in bfloat16 or wider, within the bound.
A program may use at most 128 MiB of HBM per device.

v0:
```python
import jax
import jax.numpy as jnp
from jax import lax
from jax.sharding import PartitionSpec as P

mixing = 0.5
shift_tolerance = 1e-06


def sector_mask(row_labels, column_labels):
    match = (row_labels[0][:, :, None] == column_labels[0][None, None, :]) & (
        row_labels[1][:, :, None] == column_labels[1][None, None, :]
    )
    return match.astype(jnp.float32)


def gram_of(left, right):
    column_count = left.shape[-1]
    return jnp.dot(
        left.reshape(-1, column_count).T,
        right.reshape(-1, column_count),
        precision=lax.Precision.HIGHEST,
        preferred_element_type=jnp.float32,
    )


def orthonormal(factor, values):
    column_count = values.shape[-1]
    solved = jax.scipy.linalg.solve_triangular(
        factor, values.reshape(-1, column_count).T, lower=True
    )
    return solved.T.reshape(values.shape).astype(jnp.bfloat16)


def body(
    environment, site_tensor, mpo_tensor, sketch_site, sketch_expand, row_sectors, column_sectors
):
    mpo_index = lax.axis_index("mpo")
    mpo_count = lax.axis_size("mpo")
    physical_width = environment.shape[1]
    local_rows = site_tensor.shape[0]
    physical = site_tensor.shape[1]
    column_count = column_sectors.shape[1]
    operator_rows = lax.dynamic_slice_in_dim(
        mpo_tensor, mpo_index * physical_width, physical_width, 0
    )
    sketched = jnp.einsum(
        "asb,kwb->wska", site_tensor, sketch_expand, preferred_element_type=jnp.float32
    ).astype(jnp.bfloat16)
    applied = jnp.einsum(
        "vwst,wtka->vska", mpo_tensor, sketched, preferred_element_type=jnp.float32
    ).astype(jnp.bfloat16)
    contracted = lax.all_to_all(applied, "mpo", split_axis=0, concat_axis=2, tiled=True)
    env_rows = environment
    expand_part = lax.psum_scatter(
        jnp.einsum("awc,wskc->ask", env_rows, contracted, preferred_element_type=jnp.float32),
        "bond",
        scatter_dimension=0,
        tiled=True,
    )
    mask_rows = sector_mask(row_sectors, column_sectors)
    share = local_rows // mpo_count
    offset = mpo_index * share
    expand_whole = lax.psum(expand_part, "mpo") * mask_rows
    site_whole = (
        jnp.dot(
            site_tensor.reshape(local_rows * physical, -1),
            sketch_site,
            preferred_element_type=jnp.float32,
        ).reshape(local_rows, physical, column_count)
        * mask_rows
    )
    part_site = lax.dynamic_slice_in_dim(site_whole, offset, share, 0)
    expansion_piece = lax.dynamic_slice_in_dim(expand_whole, offset, share, 0)
    square_site, square_expand = lax.psum(
        (jnp.sum(part_site * part_site), jnp.sum(expansion_piece * expansion_piece)),
        ("mpo", "bond"),
    )
    mix = mixing * jnp.sqrt((square_site + shift_tolerance) / (square_expand + shift_tolerance))
    combo_part = part_site + mix * expansion_piece
    gram_total = lax.psum(gram_of(combo_part, combo_part), ("mpo", "bond"))
    factor = jnp.linalg.cholesky(gram_total)
    basis_local = orthonormal(factor, site_whole + mix * expand_whole)
    flat_basis = basis_local.reshape(local_rows, physical * column_count)
    piece = lax.all_gather(basis_local, "bond", axis=0, tiled=True)
    env_rows = environment
    projected = jnp.einsum(
        "ax,awc->wxc",
        piece.reshape(piece.shape[0], -1),
        env_rows,
        preferred_element_type=jnp.float32,
    ).astype(jnp.bfloat16)
    couple_merged = jnp.einsum(
        "wxc,cy->wxy", projected, flat_basis, preferred_element_type=jnp.float32
    ).reshape(physical_width, physical, column_count, physical, column_count)
    boundary_share = jnp.einsum(
        "wvst,wsktl->kvl",
        operator_rows.astype(jnp.float32),
        couple_merged,
        precision=lax.Precision.HIGHEST,
    )
    reduced = lax.psum_scatter(boundary_share, "bond", scatter_dimension=0, tiled=True)
    extended = lax.psum_scatter(reduced, "mpo", scatter_dimension=1, tiled=True)
    return (basis_local, extended)


def solution(mesh):
    placed = (
        P(None, "mpo", "bond"),
        P("bond", None, None),
        P(),
        P(),
        P("mpo", None, None),
        P(None, "bond", None),
        P(),
    )
    return jax.shard_map(
        body,
        mesh=mesh,
        in_specs=placed,
        out_specs=(P("bond", None, None), P("bond", "mpo", None)),
        check_vma=False,
    )
```

profile of v0, /device:TPU:0, one launch (start us, length us, event | category | flops | bytes accessed | tf_op | source)
XLA Modules:
  0.0 739.9 jit_solution(15109001147891510651)
XLA Ops:
  7.2 31.3 %fusion.4 = bf16[32,40,512,4]{2,1,3,0:T(8,128)(2,1)} fusion(bf16[512,4,4096]{2,1,0:T(4,128)(2,1)} %param.8, bf16[32,40,4096]{2,1,0:T(8,128)(2,1)} %param.11), kind=kOutput, calls=%fused_computation.4 | convolution fusion | flops 21474836480 | bytes 32505856 | tf_op jit(solution)/shard_map/asb,kwb->wska/dot_general | solution.py:47
  38.5 4.6 fusion.13
  43.1 2.7 copy.35
  45.8 63.4 %all_to_all.18 = bf16[40,4,32,512]{3,1,2,0:T(4,128)(2,1)S(1)} all-to-all(bf16[40,4,32,512]{3,1,2,0:T(4,128)(2,1)S(1)} %copy.35), channel_id=1, replica_groups=mesh['mpo'=4,'bond'=8] {'mpo'}, dimensions={0} | all-to-all | bytes 10485760 | tf_op jit(solution)/shard_map/all_to_all | solution.py:53
  109.2 1.7 copy.36
  111.6 27.7 %fusion.10 = f32[4096,4,128]{2,0,1:T(8,128)} fusion(bf16[10,4,128,512]{3,2,0,1:T(8,128)(2,1)S(1)} %bitcast.100, bf16[4096,10,512]{2,0,1:T(8,128)(2,1)} %param.7), kind=kOutput, calls=%fused_computation.11 | convolution fusion | flops 21474836480 | bytes 55574528 | tf_op jit(solution)/shard_map/awc,wskc->ask/dot_general | solution.py:56
  139.4 148.3 %reduce-scatter.4.cloned.1.call-done = f32[512,4,128]{2,0,1:T(8,128)} async-done(((f32[4096,4,128]{2,0,1:T(8,128)}), f32[512,4,128]{2,0,1:T(8,128)}) %reduce-scatter.4.cloned.1.call-update) | async-done | bytes 1048592 | tf_op jit(solution)/shard_map/reduce_scatter | solution.py:55
  287.8 30.4 %fusion.22 = f32[512,4,128]{2,0,1:T(8,128)S(1)} fusion(bf16[512,4,4096]{2,1,0:T(4,128)(2,1)} %param.8, bf16[4096,128]{1,0:T(8,128)(2,1)S(1)} %copy-done, s32[128]{0:T(128)S(1)} %get-tuple-element.13, s32[512,4]{0,1:T(4,128)S(1)} %get-tuple-element.11, s32[128]{0:T(128)S(1)} %get-tuple-element.12, s32[512,4]{0,1:T(4,128)S(1)} %get-tuple-element.10), kind=kOutput, calls=%fused_computation.18 | convolution fusion | flops 2148532224 | bytes 18891776 | tf_op jit(solution)/shard_map/dot_general | solution.py:66
  318.9 6.6 all-reduce.4.cloned.1.call-done
  325.5 1.8 fusion.28
  327.9 40.0 %all-reduce = (f32[]{:T(128)}, f32[]{:T(128)}) all-reduce(f32[]{:T(128)} %multiply_reduce_fusion.1, f32[]{:T(128)} %multiply_reduce_fusion), channel_id=1, replica_groups=mesh['mpo'=4,'bond'=8] {'mpo','bond'}, use_global_device_ids=true, to_apply=%region_1.0 | all-reduce | flops 2 | bytes 16 | tf_op jit(solution)/shard_map/psum | solution.py:75
  369.3 1.2 convolution_bitcast_fusion
  370.8 119.7 %all-reduce.6.cloned.1.call-done = f32[128,128]{0,1:T(8,128)} async-done(((f32[128,128]{0,1:T(8,128)}), f32[128,128]{0,1:T(8,128)}) %all-reduce.6.cloned.1.call-update) | async-done | bytes 65552 | tf_op jit(solution)/shard_map/psum | solution.py:81
  492.3 11.7 %cholesky.16 = f32[128,128]{1,0:T(8,128)S(1)} custom-call(f32[128,128]{1,0:T(8,128)S(1)} %fusion.41), custom_call_target="Cholesky" | custom-call | tf_op jit(solution)/shard_map/jit(cholesky)/cholesky | solution.py:82
  505.4 9.8 %custom-call.7 = f32[1,128,128]{1,2,0:T(8,128)S(1)} custom-call(f32[1,128,128]{2,1,0:T(8,128)S(1)} %fusion.38), custom_call_target="InvertDiagBlocksLowerTriangular" | custom-call | tf_op jit(solution)/shard_map/jit(_solve_triangular)/triangular_solve | solution.py:29
  515.2 2.0 convolution_convert_fusion.1
  517.3 75.9 %all-gather.2.cloned.1.call-done = bf16[4096,4,128]{0,2,1:T(8,128)(2,1)} async-done(((bf16[512,4,128]{0,2,1:T(8,128)(2,1)}), bf16[4096,4,128]{0,2,1:T(8,128)(2,1)}) %all-gather.2.cloned.1.call-update) | async-done | bytes 4194320 | tf_op jit(solution)/shard_map/all_gather | solution.py:85
  593.2 27.9 %convolution_convert_fusion = bf16[512,10,512]{2,0,1:T(8,128)(2,1)S(1)} fusion(bf16[4096,512,1]{0,1,2:T(8,128)(2,1)} %bitcast.101, bf16[4096,10,512]{2,0,1:T(8,128)(2,1)} %param.7), kind=kOutput, calls=%fused_computation.16 | convolution fusion | flops 21477457920 | bytes 51380224 | tf_op jit(solution)/shard_map/ax,awc->wxc/dot_general | solution.py:87
  621.1 2.9 fusion.29
  624.0 16.9 %fusion.19 = f32[128,40,128]{2,1,0:T(8,128)} fusion(f32[10,4,128,4,128]{4,2,3,1,0:T(8,128)S(1)} %fusion.29, bf16[40,40,4,4]{1,0,3,2:T(8,128)(2,1)S(1)} %copy.34, s32[]{:T(128)S(6)} %select_n.13), kind=kOutput, calls=%fused_computation.17 | convolution fusion | flops 1258291200 | bytes 13172740 | tf_op jit(solution)/shard_map/wvst,wsktl->kvl/dot_general | solution.py:96
  640.9 69.2 %reduce-scatter.6.cloned.1.call-done = f32[16,40,128]{2,1,0:T(8,128)} async-done(((f32[128,40,128]{2,1,0:T(8,128)}), f32[16,40,128]{2,1,0:T(8,128)}) %reduce-scatter.6.cloned.1.call-update) | async-done | bytes 327696 | tf_op jit(solution)/shard_map/reduce_scatter | solution.py:102
  710.2 1.7 copy.45
  711.9 1.1 copy.46
  713.0 19.7 %reduce-scatter.8.cloned.1.call-done = f32[16,10,128]{2,0,1:T(8,128)} async-done(((f32[16,40,128]{2,0,1:T(8,128)}), f32[16,10,128]{2,0,1:T(8,128)}) %reduce-scatter.8.cloned.1.call-update) | async-done | bytes 81936 | tf_op jit(solution)/shard_map/reduce_scatter | solution.py:103
  (33 shorter events, 5.7 us)
Async XLA Ops:
  7.2 280.6 %copy-start = (bf16[4096,128]{1,0:T(8,128)(2,1)S(1)}, bf16[4096,128]{1,0:T(8,128)(2,1)}, u32[]{:S(2)}) copy-start(bf16[4096,128]{1,0:T(8,128)(2,1)} %param.10) | copy-start | bytes 3145732
  7.2 31.4 %copy-start.2 = (bf16[40,40,4,4]{1,3,2,0:T(4,128)(2,1)S(1)}, bf16[40,40,4,4]{1,3,2,0:T(4,128)(2,1)}, u32[]{:S(2)}) copy-start(bf16[40,40,4,4]{1,3,2,0:T(4,128)(2,1)} %param.9) | copy-start | bytes 153604
  7.2 280.5 %reduce-scatter.4.cloned.1.call-start = ((), (), s32[]{:S(2)}) async-start(), calls=%async_computation.4 | async-start | bytes 9437184 | tf_op jit(solution)/shard_map/reduce_scatter | solution.py:55
  111.6 27.8 %copy-start.4 = (s32[2,128]{1,0:T(2,128)S(1)}, s32[2,128]{1,0:T(2,128)}, u32[]{:S(2)}) copy-start(s32[2,128]{1,0:T(2,128)} %param.13) | copy-start | bytes 3076
  111.6 27.8 %copy-start.3 = (s32[2,512,4]{1,2,0:T(4,128)S(1)}, s32[2,512,4]{1,2,0:T(4,128)}, u32[]{:S(2)}) copy-start(s32[2,512,4]{1,2,0:T(4,128)} %param.12) | copy-start | bytes 49156
  139.3 186.1 %all-reduce.4.cloned.1.call-start = ((), (), s32[]{:S(2)}) async-start(), calls=%async_computation.5 | async-start | bytes 2097152 | tf_op jit(solution)/shard_map/psum | solution.py:64
  287.7 202.8 %all-reduce.6.cloned.1.call-start = ((), (), s32[]{:S(2)}) async-start(), calls=%async_computation.6 | async-start | bytes 131072 | tf_op jit(solution)/shard_map/psum | solution.py:81
  370.6 222.6 %all-gather.2.cloned.1.call-start = ((), (), s32[]{:S(2)}) async-start(), calls=%async_computation.7 | async-start | bytes 4718592 | tf_op jit(solution)/shard_map/all_gather | solution.py:85
  517.2 193.0 %reduce-scatter.6.cloned.1.call-start = ((), (), s32[]{:S(2)}) async-start(), calls=%async_computation.8 | async-start | bytes 2949120 | tf_op jit(solution)/shard_map/reduce_scatter | solution.py:102
  593.2 27.9 %copy-start.1 = (bf16[512,4,128]{0,2,1:T(8,128)(2,1)S(1)}, bf16[512,4,128]{0,2,1:T(8,128)(2,1)}, u32[]{:S(2)}) copy-start(bf16[512,4,128]{0,2,1:T(8,128)(2,1)} %convolution_convert_fusion.1) | copy-start | bytes 1572868
  640.9 91.8 %reduce-scatter.8.cloned.1.call-start = ((), (), s32[]{:S(2)}) async-start(), calls=%async_computation.9 | async-start | bytes 409600 | tf_op jit(solution)/shard_map/reduce_scatter | solution.py:103
Sparse Core Ops, SparseCore 0:
  139.5 148.2 reduce-scatter.3
  290.1 35.3 all-reduce.3
  370.7 119.7 all-reduce.5
  517.3 75.8 all-gather.1
  641.0 69.0 reduce-scatter.5
  713.1 19.5 reduce-scatter.7
where the time goes:
time: 749 us; the launch traced here: 740 us
  waiting for transfers between devices  439 us (59%)
  matrix products  145 us (19%)
  blocking collectives  103 us (14%)
  other arithmetic  26.8 us (4%)
  between operations  16.1 us (2%)
  local copies, waits for them, and re-layouts  8.83 us (1%)
    reduce_scatter x1, waiting for transfers between devices, body(): lax.psum_scatter(jnp.einsum('awc,wskc->ask', env_rows, contracted, prefer...  148 us
    psum x1, waiting for transfers between devices, body(): gram_total = lax.psum(gram_of(combo_part, combo_part), ('mpo', 'bond'))  120 us
    all_gather x1, waiting for transfers between devices, body(): piece = lax.all_gather(basis_local, 'bond', axis=0, tiled=True)  75.9 us
    reduce_scatter x1, waiting for transfers between devices, body(): lax.psum_scatter(boundary_share, 'bond', scatter_dimension=0, tiled=True)  69.2 us
    all_to_all x1, blocking collectives, body(): lax.all_to_all(applied, 'mpo', split_axis=0, concat_axis=2, tiled=True)  63.4 us
    psum x1, blocking collectives, body(): lax.psum((jnp.sum(part_site * part_site), jnp.sum(expansion_piece * expan...  40 us
    dot_general x1, matrix products, body(): jnp.einsum('asb,kwb->wska', site_tensor, sketch_expand, preferred_element...  31.3 us
    dot_general x1, matrix products, body(): jnp.dot(site_tensor.reshape(local_rows * physical, -1), sketch_site, pref...  30.4 us
  transfers between devices with their start and end apart: 6, of which 6 were waited for; matrix products, arithmetic and copies ran while one was open for 4% of the time, Pallas kernels for 0%

commit v1 on v0

--- a/solution.py
+++ b/solution.py
@@ -78,7 +78,7 @@
     )
     mix = mixing * jnp.sqrt((square_site + shift_tolerance) / (square_expand + shift_tolerance))
     combo_part = part_site + mix * expansion_piece
-    gram_total = lax.psum(gram_of(combo_part, combo_part), ("mpo", "bond"))
+    gram_total = jnp.sum(lax.all_gather(gram_of(combo_part, combo_part), ("mpo", "bond")), axis=0)
     factor = jnp.linalg.cholesky(gram_total)
     basis_local = orthonormal(factor, site_whole + mix * expand_whole)
     flat_basis = basis_local.reshape(local_rows, physical * column_count)

time: 749 us -> 683 us (0.912)
  waiting for transfers between devices: 439 us -> 374 us
    psum x1 -> x0, waiting for transfers between devices: 120 us -> none  [body(): gram_total = lax.psum(gram_of(combo_part, combo_part), ('mpo', 'bond'))]
    all_gather x0 -> x1, waiting for transfers between devices: none -> 56.7 us  [body(): lax.all_gather(gram_of(combo_part, combo_part), ('mpo', 'bond'))]
  transfers between devices with their start and end apart: 6 -> 6, of which waited for: 6 -> 6; matrix products, arithmetic and copies ran while one was open for 4% -> 5% of each run, Pallas kernels for 0% -> 0%
where the time goes in v1:
time: 683 us; the launch traced here: 675 us
  waiting for transfers between devices  374 us (55%)
  matrix products  145 us (21%)
  blocking collectives  103 us (15%)
  other arithmetic  27.7 us (4%)
  between operations  16.1 us (2%)
  local copies, waits for them, and re-layouts  7.99 us (1%)
    reduce_scatter x1, waiting for transfers between devices, body(): lax.psum_scatter(jnp.einsum('awc,wskc->ask', env_rows, contracted, prefer...  148 us
    all_gather x1, waiting for transfers between devices, body(): piece = lax.all_gather(basis_local, 'bond', axis=0, tiled=True)  73.5 us
    reduce_scatter x1, waiting for transfers between devices, body(): lax.psum_scatter(boundary_share, 'bond', scatter_dimension=0, tiled=True)  69.4 us
    all_to_all x1, blocking collectives, body(): lax.all_to_all(applied, 'mpo', split_axis=0, concat_axis=2, tiled=True)  63.4 us
    all_gather x1, waiting for transfers between devices, body(): lax.all_gather(gram_of(combo_part, combo_part), ('mpo', 'bond'))  56.7 us
    psum x1, blocking collectives, body(): lax.psum((jnp.sum(part_site * part_site), jnp.sum(expansion_piece * expan...  40 us
    dot_general x1, matrix products, body(): jnp.einsum('asb,kwb->wska', site_tensor, sketch_expand, preferred_element...  31.3 us
    dot_general x1, matrix products, body(): jnp.dot(site_tensor.reshape(local_rows * physical, -1), sketch_site, pref...  30.4 us
  transfers between devices with their start and end apart: 6, of which 6 were waited for; matrix products, arithmetic and copies ran while one was open for 5% of the time, Pallas kernels for 0%

profile of v1, /device:TPU:0, one launch (start us, length us, event | category | flops | bytes accessed | tf_op | source)
XLA Modules:
  0.0 674.7 jit_solution(15912210380041272262)
XLA Ops:
  7.2 31.3 %fusion.4 = bf16[32,40,512,4]{2,1,3,0:T(8,128)(2,1)} fusion(bf16[512,4,4096]{2,1,0:T(4,128)(2,1)} %param.8, bf16[32,40,4096]{2,1,0:T(8,128)(2,1)} %param.11), kind=kOutput, calls=%fused_computation.4 | convolution fusion | flops 21474836480 | bytes 32505856 | tf_op jit(solution)/shard_map/asb,kwb->wska/dot_general | solution.py:47
  38.5 4.6 fusion.13
  43.1 2.7 copy.33
  45.8 63.4 %all_to_all.18 = bf16[40,4,32,512]{3,1,2,0:T(4,128)(2,1)S(1)} all-to-all(bf16[40,4,32,512]{3,1,2,0:T(4,128)(2,1)S(1)} %copy.33), channel_id=1, replica_groups=mesh['mpo'=4,'bond'=8] {'mpo'}, dimensions={0} | all-to-all | bytes 10485760 | tf_op jit(solution)/shard_map/all_to_all | solution.py:53
  109.2 1.7 copy.34
  111.6 27.7 %fusion.10 = f32[4096,4,128]{2,0,1:T(8,128)} fusion(bf16[10,4,128,512]{3,2,0,1:T(8,128)(2,1)S(1)} %bitcast.101, bf16[4096,10,512]{2,0,1:T(8,128)(2,1)} %param.7), kind=kOutput, calls=%fused_computation.11 | convolution fusion | flops 21474836480 | bytes 55574528 | tf_op jit(solution)/shard_map/awc,wskc->ask/dot_general | solution.py:56
  139.4 148.3 %reduce-scatter.4.cloned.1.call-done = f32[512,4,128]{2,0,1:T(8,128)} async-done(((f32[4096,4,128]{2,0,1:T(8,128)}), f32[512,4,128]{2,0,1:T(8,128)}) %reduce-scatter.4.cloned.1.call-update) | async-done | bytes 1048592 | tf_op jit(solution)/shard_map/reduce_scatter | solution.py:55
  287.8 30.4 %fusion.22 = f32[512,4,128]{2,0,1:T(8,128)S(1)} fusion(bf16[512,4,4096]{2,1,0:T(4,128)(2,1)} %param.8, bf16[4096,128]{1,0:T(8,128)(2,1)S(1)} %copy-done, s32[128]{0:T(128)S(1)} %get-tuple-element.13, s32[512,4]{0,1:T(4,128)S(1)} %get-tuple-element.11, s32[128]{0:T(128)S(1)} %get-tuple-element.12, s32[512,4]{0,1:T(4,128)S(1)} %get-tuple-element.10), kind=kOutput, calls=%fused_computation.18 | convolution fusion | flops 2148532224 | bytes 18891776 | tf_op jit(solution)/shard_map/dot_general | solution.py:66
  318.9 6.6 all-reduce.3.cloned.1.call-done
  325.5 1.8 fusion.28
  327.9 40.0 %all-reduce = (f32[]{:T(128)}, f32[]{:T(128)}) all-reduce(f32[]{:T(128)} %multiply_reduce_fusion.1, f32[]{:T(128)} %multiply_reduce_fusion), channel_id=1, replica_groups=mesh['mpo'=4,'bond'=8] {'mpo','bond'}, use_global_device_ids=true, to_apply=%region_1.0 | all-reduce | flops 2 | bytes 16 | tf_op jit(solution)/shard_map/psum | solution.py:75
  369.3 1.2 convolution_bitcast_fusion
  370.8 56.7 %all-gather.6.cloned.1.call-done = f32[4096,128]{1,0:T(8,128)} async-done(((f32[128,128]{1,0:T(8,128)}), f32[4096,128]{1,0:T(8,128)}) %all-gather.6.cloned.1.call-update) | async-done | bytes 2097168 | tf_op jit(solution)/shard_map/all_gather | solution.py:81
  427.5 1.7 reduce_sum.29
  429.3 11.7 %cholesky.16 = f32[128,128]{1,0:T(8,128)S(1)} custom-call(f32[128,128]{1,0:T(8,128)S(1)} %fusion.41), custom_call_target="Cholesky" | custom-call | tf_op jit(solution)/shard_map/jit(cholesky)/cholesky | solution.py:82
  442.3 9.8 %custom-call.7 = f32[1,128,128]{1,2,0:T(8,128)S(1)} custom-call(f32[1,128,128]{2,1,0:T(8,128)S(1)} %fusion.38), custom_call_target="InvertDiagBlocksLowerTriangular" | custom-call | tf_op jit(solution)/shard_map/jit(_solve_triangular)/triangular_solve | solution.py:29
  452.1 2.0 convolution_convert_fusion.1
  454.2 73.5 %all-gather.4.cloned.1.call-done = bf16[4096,4,128]{0,2,1:T(8,128)(2,1)} async-done(((bf16[512,4,128]{0,2,1:T(8,128)(2,1)}), bf16[4096,4,128]{0,2,1:T(8,128)(2,1)}) %all-gather.4.cloned.1.call-update) | async-done | bytes 4194320 | tf_op jit(solution)/shard_map/all_gather | solution.py:85
  527.8 27.9 %convolution_convert_fusion = bf16[512,10,512]{2,0,1:T(8,128)(2,1)S(1)} fusion(bf16[4096,512,1]{0,1,2:T(8,128)(2,1)} %bitcast.103, bf16[4096,10,512]{2,0,1:T(8,128)(2,1)} %param.7), kind=kOutput, calls=%fused_computation.16 | convolution fusion | flops 21477457920 | bytes 51380224 | tf_op jit(solution)/shard_map/ax,awc->wxc/dot_general | solution.py:87
  555.7 2.9 fusion.29
  558.6 16.9 %fusion.19 = f32[128,40,128]{2,1,0:T(8,128)} fusion(f32[10,4,128,4,128]{4,2,3,1,0:T(8,128)S(1)} %fusion.29, bf16[40,40,4,4]{1,0,3,2:T(8,128)(2,1)S(1)} %copy.32, s32[]{:T(128)S(6)} %select_n.13), kind=kOutput, calls=%fused_computation.17 | convolution fusion | flops 1258291200 | bytes 13172740 | tf_op jit(solution)/shard_map/wvst,wsktl->kvl/dot_general | solution.py:96
  575.5 69.4 %reduce-scatter.6.cloned.1.call-done = f32[16,40,128]{2,1,0:T(8,128)} async-done(((f32[128,40,128]{2,1,0:T(8,128)}), f32[16,40,128]{2,1,0:T(8,128)}) %reduce-scatter.6.cloned.1.call-update) | async-done | bytes 327696 | tf_op jit(solution)/shard_map/reduce_scatter | solution.py:102
  644.9 1.7 copy.42
  647.7 19.7 %reduce-scatter.8.cloned.1.call-done = f32[16,10,128]{2,0,1:T(8,128)} async-done(((f32[16,40,128]{2,0,1:T(8,128)}), f32[16,10,128]{2,0,1:T(8,128)}) %reduce-scatter.8.cloned.1.call-update) | async-done | bytes 81936 | tf_op jit(solution)/shard_map/reduce_scatter | solution.py:103
  (34 shorter events, 5.1 us)
Async XLA Ops:
  7.2 280.6 %copy-start = (bf16[4096,128]{1,0:T(8,128)(2,1)S(1)}, bf16[4096,128]{1,0:T(8,128)(2,1)}, u32[]{:S(2)}) copy-start(bf16[4096,128]{1,0:T(8,128)(2,1)} %param.10) | copy-start | bytes 3145732
  7.2 31.4 %copy-start.2 = (bf16[40,40,4,4]{1,3,2,0:T(4,128)(2,1)S(1)}, bf16[40,40,4,4]{1,3,2,0:T(4,128)(2,1)}, u32[]{:S(2)}) copy-start(bf16[40,40,4,4]{1,3,2,0:T(4,128)(2,1)} %param.9) | copy-start | bytes 153604
  7.2 280.5 %reduce-scatter.4.cloned.1.call-start = ((), (), s32[]{:S(2)}) async-start(), calls=%async_computation.4 | async-start | bytes 9437184 | tf_op jit(solution)/shard_map/reduce_scatter | solution.py:55
  111.6 27.8 %copy-start.4 = (s32[2,128]{1,0:T(2,128)S(1)}, s32[2,128]{1,0:T(2,128)}, u32[]{:S(2)}) copy-start(s32[2,128]{1,0:T(2,128)} %param.13) | copy-start | bytes 3076
  111.6 27.8 %copy-start.3 = (s32[2,512,4]{1,2,0:T(4,128)S(1)}, s32[2,512,4]{1,2,0:T(4,128)}, u32[]{:S(2)}) copy-start(s32[2,512,4]{1,2,0:T(4,128)} %param.12) | copy-start | bytes 49156
  139.3 186.1 %all-reduce.3.cloned.1.call-start = ((), (), s32[]{:S(2)}) async-start(), calls=%async_computation.5 | async-start | bytes 2097152 | tf_op jit(solution)/shard_map/psum | solution.py:64
  287.7 139.7 %all-gather.6.cloned.1.call-start = ((), (), s32[]{:S(2)}) async-start(), calls=%async_computation.9 | async-start | bytes 2162688 | tf_op jit(solution)/shard_map/all_gather | solution.py:81
  370.6 157.2 %all-gather.4.cloned.1.call-start = ((), (), s32[]{:S(2)}) async-start(), calls=%async_computation.6 | async-start | bytes 4718592 | tf_op jit(solution)/shard_map/all_gather | solution.py:85
  454.1 190.8 %reduce-scatter.6.cloned.1.call-start = ((), (), s32[]{:S(2)}) async-start(), calls=%async_computation.7 | async-start | bytes 2949120 | tf_op jit(solution)/shard_map/reduce_scatter | solution.py:102
  527.8 27.9 %copy-start.1 = (bf16[512,4,128]{0,2,1:T(8,128)(2,1)S(1)}, bf16[512,4,128]{0,2,1:T(8,128)(2,1)}, u32[]{:S(2)}) copy-start(bf16[512,4,128]{0,2,1:T(8,128)(2,1)} %convolution_convert_fusion.1) | copy-start | bytes 1572868
  575.5 91.9 %reduce-scatter.8.cloned.1.call-start = ((), (), s32[]{:S(2)}) async-start(), calls=%async_computation.8 | async-start | bytes 409600 | tf_op jit(solution)/shard_map/reduce_scatter | solution.py:103
Sparse Core Ops, SparseCore 0:
  139.5 148.2 reduce-scatter.3
  290.1 35.3 all-reduce.2
  370.7 56.7 all-gather.5
  454.3 73.4 all-gather.3
  575.6 69.2 reduce-scatter.5
  647.8 19.5 reduce-scatter.7
